TPU v7x, 32 devices: a whole 2x2x4 slice. The times are simulated.
32 devices in a mesh: batch: 8 (over z, x), head: 4 (over y, core).
Axes of the slice: x: 2, y: 2, z: 4, core: 2. Of those that a mesh axis runs over, the one named last changes fastest.
Arguments:
- tokens: bfloat16 [16384, 768], P(('batch', 'head')), may hold values from -6 to 6
- cotangent: bfloat16 [16384, 768], P(('batch', 'head')), may hold values from -6 to 6
- lengths: int32 [8, 3], P('batch'), may hold values from 1 to 1024, 2048 in all within a row
- input_weight: float32 [2304, 768], P(('batch', 'head')), may hold values from -0.21875 to 0.21875
- output_weight: float32 [768, 768], P(('batch', 'head')), may hold values from -0.875 to 0.875
- expand_weight: float32 [3072, 768], P(('batch', 'head')), may hold values from -0.21875 to 0.21875
- contract_weight: float32 [768, 3072], P(('batch', 'head')), may hold values from -0.109375 to 0.109375
- vector_params: float32 [9216], replicated, may hold values from -0.8 to 1.6, as said below
- input_first: float32 [2304, 768], P(('batch', 'head')), may hold values from -0.005859375 to 0.005859375
- input_second: float32 [2304, 768], P(('batch', 'head')), may hold values from 1.4128508e-07 to 5.6514034e-07
- output_first: float32 [768, 768], P(('batch', 'head')), may hold values from -0.005859375 to 0.005859375
- output_second: float32 [768, 768], P(('batch', 'head')), may hold values from 1.4128508e-07 to 5.6514034e-07
- expand_first: float32 [3072, 768], P(('batch', 'head')), may hold values from -0.005859375 to 0.005859375
- expand_second: float32 [3072, 768], P(('batch', 'head')), may hold values from 1.4128508e-07 to 5.6514034e-07
- contract_first: float32 [768, 3072], P(('batch', 'head')), may hold values from -0.005859375 to 0.005859375
- contract_second: float32 [768, 3072], P(('batch', 'head')), may hold values from 1.4128508e-07 to 5.6514034e-07
- vector_first: float32 [9216], replicated, may hold values from -0.0234375 to 0.0234375
- vector_second: float32 [9216], replicated, may hold values from 2.2605614e-06 to 9.042245e-06
Outputs:
- block_out: bfloat16 [16384, 768], P(('batch', 'head'))
- input_grad: bfloat16 [16384, 768], P(('batch', 'head'))
- grad_norm: float32 [], replicated
- matrix_norms: float32 [8], replicated
- input_first_new: float32 [2304, 768], P(('batch', 'head'))
- input_second_new: float32 [2304, 768], P(('batch', 'head'))
- input_weight_new: float32 [2304, 768], P(('batch', 'head'))
- input_weight_low: bfloat16 [2304, 768], P(('batch', 'head'))
- output_first_new: float32 [768, 768], P(('batch', 'head'))
- output_second_new: float32 [768, 768], P(('batch', 'head'))
- output_weight_new: float32 [768, 768], P(('batch', 'head'))
- output_weight_low: bfloat16 [768, 768], P(('batch', 'head'))
- expand_first_new: float32 [3072, 768], P(('batch', 'head'))
- expand_second_new: float32 [3072, 768], P(('batch', 'head'))
- expand_weight_new: float32 [3072, 768], P(('batch', 'head'))
- expand_weight_low: bfloat16 [3072, 768], P(('batch', 'head'))
- contract_first_new: float32 [768, 3072], P(('batch', 'head'))
- contract_second_new: float32 [768, 3072], P(('batch', 'head'))
- contract_weight_new: float32 [768, 3072], P(('batch', 'head'))
- contract_weight_low: bfloat16 [768, 3072], P(('batch', 'head'))
- vector_first_new: float32 [9216], replicated
- vector_second_new: float32 [9216], replicated
- vector_params_new: float32 [9216], replicated
Inputs may be any that keep to these rules, and one draw needn't show every extreme that they name: Each row holds 3 lengths summing to 2048; the longest in every row is exactly half of 2048. `vector_params`: entries 0 to 767 and 1536 to 2303 are norm gains near 1; the rest are shifts and biases.
All inputs are finite; a program needn't handle non-finite values.
Results may differ from a plain program's by a relative error of at most 0.012.
Values may be sent and summed in bfloat16 or wider, within the bound.
No kernel may reach another device: no remote copies, remote signals or barrier semaphores. Data moves between devices by JAX's collectives and lax.ppermute only.
A program may use at most 192 MiB of HBM per device.

v0:
```python
from functools import partial
import jax
import jax.numpy as jnp
from jax import lax
from jax.sharding import PartitionSpec as P

D = 768
HD = 64
FF = 3072
STEP = 5
NORM_EPS = 1e-05
ADAM_EPS = 1e-06
DECAY_RATE = 0.01
MATRIX_RATE = 0.5
VECTOR_RATE = 0.1


def layer_norm(values, gain_vec, bias_vec):
    row_mean = jnp.mean(values, axis=-1, keepdims=True)
    centered = values - row_mean
    variance = jnp.mean(centered * centered, axis=-1, keepdims=True)
    return centered * lax.rsqrt(variance + NORM_EPS) * gain_vec + bias_vec


def unpack_vector(params):
    pieces = [params[position * D : (position + 1) * D] for position in range(8)]
    return pieces + [params[8 * D : 8 * D + FF]]


def masked_scores(query_block, key_rows, segment, offset, block_rows, score_scale):
    scores = (
        jnp.einsum("qhd,khd->hqk", query_block, key_rows, preferred_element_type=jnp.float32)
        * score_scale
    )
    query_pos = offset + jnp.arange(block_rows, dtype=jnp.int32)
    key_pos = jnp.arange(key_rows.shape[0], dtype=jnp.int32)
    query_seg = lax.dynamic_slice_in_dim(segment, offset, block_rows, 0)
    allowed = (key_pos[None, :] <= query_pos[:, None]) & (query_seg[:, None] == segment[None, :])
    return jnp.where(allowed[None], scores, -1e30)


def head_forward(head_inputs, segment, block_count, block_rows, score_scale):
    group_rows = head_inputs.shape[1]
    heads_here = head_inputs.shape[2] // HD
    queries = head_inputs[0].reshape(group_rows, heads_here, HD)
    key_rows = head_inputs[1].reshape(group_rows, heads_here, HD)
    value_rows = head_inputs[2].reshape(group_rows, heads_here, HD)

    def one_block(block_index):
        offset = block_index * block_rows
        query_block = lax.dynamic_slice_in_dim(queries, offset, block_rows, 0)
        scores = masked_scores(query_block, key_rows, segment, offset, block_rows, score_scale)
        row_max = jnp.max(scores, axis=-1, keepdims=True)
        exponent = jnp.exp(scores - row_max)
        row_total = jnp.sum(exponent, axis=-1, keepdims=True)
        soft_weights = (exponent / row_total).astype(jnp.bfloat16)
        attended = jnp.einsum(
            "hqk,khd->qhd", soft_weights, value_rows, preferred_element_type=jnp.float32
        )
        return (attended.astype(jnp.bfloat16), row_max + jnp.log(row_total))

    attended, log_totals = lax.map(one_block, jnp.arange(block_count, dtype=jnp.int32))
    return (attended.reshape(group_rows, heads_here * HD), log_totals)


def head_backward(
    head_inputs, grad_heads, log_totals, segment, block_count, block_rows, score_scale
):
    group_rows = head_inputs.shape[1]
    heads_here = head_inputs.shape[2] // HD
    queries = head_inputs[0].reshape(group_rows, heads_here, HD)
    key_rows = head_inputs[1].reshape(group_rows, heads_here, HD)
    value_rows = head_inputs[2].reshape(group_rows, heads_here, HD)
    grad_out = grad_heads.reshape(group_rows, heads_here, HD)

    def one_block(state_pair, scan_item):
        grad_keys, grad_values = state_pair
        block_index, block_logs = scan_item
        offset = block_index * block_rows
        query_block = lax.dynamic_slice_in_dim(queries, offset, block_rows, 0)
        grad_block = lax.dynamic_slice_in_dim(grad_out, offset, block_rows, 0)
        scores = masked_scores(query_block, key_rows, segment, offset, block_rows, score_scale)
        probs = jnp.exp(scores - block_logs)
        grad_values = grad_values + jnp.einsum(
            "hqk,qhd->khd",
            probs.astype(jnp.bfloat16),
            grad_block,
            preferred_element_type=jnp.float32,
        )
        grad_probs = jnp.einsum(
            "qhd,khd->hqk", grad_block, value_rows, preferred_element_type=jnp.float32
        )
        row_delta = jnp.sum(probs * grad_probs, axis=-1, keepdims=True)
        grad_scores = (probs * (grad_probs - row_delta)).astype(jnp.bfloat16)
        grad_queries = (
            jnp.einsum("hqk,khd->qhd", grad_scores, key_rows, preferred_element_type=jnp.float32)
            * score_scale
        )
        grad_keys = (
            grad_keys
            + jnp.einsum(
                "hqk,qhd->khd", grad_scores, query_block, preferred_element_type=jnp.float32
            )
            * score_scale
        )
        return ((grad_keys, grad_values), grad_queries)

    zero_state = jnp.zeros((group_rows, heads_here, HD), jnp.float32)
    final_state, grad_queries = lax.scan(
        one_block, (zero_state, zero_state), (jnp.arange(block_count, dtype=jnp.int32), log_totals)
    )
    width_here = heads_here * HD
    stacked = jnp.stack(
        [
            grad_queries.reshape(group_rows, width_here),
            final_state[0].reshape(group_rows, width_here),
            final_state[1].reshape(group_rows, width_here),
        ]
    )
    return stacked.astype(jnp.bfloat16)


def adam_direction(gradient, first_old, second_old, master, clip_factor):
    clipped = gradient * clip_factor
    first_new = 0.5 * first_old + 0.5 * clipped
    second_new = 0.5 * second_old + 0.5 * clipped * clipped
    correction = 1.0 - 0.5**STEP
    direction = (
        first_new / correction / (jnp.sqrt(second_new / correction) + ADAM_EPS)
        + DECAY_RATE * master
    )
    return (first_new, second_new, direction)


def on_device(
    tokens,
    cotangent,
    lengths,
    input_weight,
    output_weight,
    expand_weight,
    contract_weight,
    vector_params,
    input_first,
    input_second,
    output_first,
    output_second,
    expand_first,
    expand_second,
    contract_first,
    contract_second,
    vector_first,
    vector_second,
):
    head_count = lax.axis_size("head")
    local_rows = tokens.shape[0]
    group_rows = local_rows * head_count
    block_rows = min(512, group_rows)
    block_count = group_rows // block_rows
    score_scale = HD ** (-0.5)
    (
        gain_one,
        bias_one,
        gain_two,
        bias_two,
        bias_query,
        bias_value,
        bias_output,
        bias_contract,
        bias_expand,
    ) = unpack_vector(vector_params)
    full_input, full_output, full_expand, full_contract = (
        lax.all_gather(input_weight.astype(jnp.bfloat16), ("batch", "head"), axis=0, tiled=True),
        lax.all_gather(output_weight.astype(jnp.bfloat16), ("batch", "head"), axis=0, tiled=True),
        lax.all_gather(expand_weight.astype(jnp.bfloat16), ("batch", "head"), axis=0, tiled=True),
        lax.all_gather(contract_weight.astype(jnp.bfloat16), ("batch", "head"), axis=0, tiled=True),
    )
    stacked_input = full_input.reshape(3, D, D)
    doc_ends = jnp.stack(
        [jnp.sum(lengths[0, : position + 1]) for position in range(lengths.shape[1])]
    )
    positions = jnp.arange(group_rows, dtype=jnp.int32)
    segment = jnp.sum((positions[:, None] >= doc_ends[None, :]).astype(jnp.int32), axis=1)
    resid_in = tokens.astype(jnp.float32)
    normed_one = layer_norm(resid_in, gain_one, bias_one).astype(jnp.bfloat16)
    input_bias = jnp.stack([bias_query, jnp.zeros_like(bias_query), bias_value])[:, None, :]
    projected = (
        jnp.einsum("td,cod->cto", normed_one, stacked_input, preferred_element_type=jnp.float32)
        + input_bias
    ).astype(jnp.bfloat16)
    head_inputs = lax.all_to_all(projected, "head", split_axis=2, concat_axis=1, tiled=True)
    head_out, log_totals = head_forward(head_inputs, segment, block_count, block_rows, score_scale)
    attended = lax.all_to_all(head_out, "head", split_axis=0, concat_axis=1, tiled=True)
    branch = (
        jnp.einsum("tc,oc->to", attended, full_output, preferred_element_type=jnp.float32)
        + bias_output
    )
    resid_mid = resid_in + branch
    normed_two = layer_norm(resid_mid, gain_two, bias_two).astype(jnp.bfloat16)
    expanded = (
        jnp.einsum("td,fd->tf", normed_two, full_expand, preferred_element_type=jnp.float32)
        + bias_expand
    )
    activated = jax.nn.gelu(expanded, approximate=True).astype(jnp.bfloat16)
    block_out = (
        resid_mid
        + jnp.einsum("tf,of->to", activated, full_contract, preferred_element_type=jnp.float32)
        + bias_contract
    ).astype(jnp.bfloat16)
    upstream = cotangent.astype(jnp.float32)
    grad_contract = jnp.einsum(
        "to,tf->of", cotangent, activated, preferred_element_type=jnp.float32
    )
    grad_activated = jnp.einsum(
        "to,of->tf", cotangent, full_contract, preferred_element_type=jnp.float32
    )
    unused_gelu, gelu_pull = jax.vjp(partial(jax.nn.gelu, approximate=True), expanded)
    grad_expanded = gelu_pull(grad_activated)[0].astype(jnp.bfloat16)
    grad_expand = jnp.einsum(
        "tf,td->fd", grad_expanded, normed_two, preferred_element_type=jnp.float32
    )
    grad_normed_two = jnp.einsum(
        "tf,fd->td", grad_expanded, full_expand, preferred_element_type=jnp.float32
    )
    unused_second, norm_pull_two = jax.vjp(layer_norm, resid_mid, gain_two, bias_two)
    grad_mid_norm, grad_gain_two, grad_bias_two = norm_pull_two(grad_normed_two)
    grad_mid = upstream + grad_mid_norm
    grad_branch = grad_mid.astype(jnp.bfloat16)
    grad_output = jnp.einsum("to,tc->oc", grad_branch, attended, preferred_element_type=jnp.float32)
    grad_attended = jnp.einsum(
        "to,oc->tc", grad_branch, full_output, preferred_element_type=jnp.float32
    ).astype(jnp.bfloat16)
    grad_heads = lax.all_to_all(grad_attended, "head", split_axis=1, concat_axis=0, tiled=True)
    grad_projected_heads = head_backward(
        head_inputs, grad_heads, log_totals, segment, block_count, block_rows, score_scale
    )
    grad_projected = lax.all_to_all(
        grad_projected_heads, "head", split_axis=1, concat_axis=2, tiled=True
    )
    grad_input = jnp.einsum(
        "cto,td->cod", grad_projected, normed_one, preferred_element_type=jnp.float32
    ).reshape(3 * D, D)
    grad_normed_one = jnp.einsum(
        "cto,cod->td", grad_projected, stacked_input, preferred_element_type=jnp.float32
    )
    unused_first, norm_pull_one = jax.vjp(layer_norm, resid_in, gain_one, bias_one)
    grad_in_norm, grad_gain_one, grad_bias_one = norm_pull_one(grad_normed_one)
    input_grad = (grad_mid + grad_in_norm).astype(jnp.bfloat16)
    projected_sums = jnp.sum(grad_projected.astype(jnp.float32), axis=1)
    vector_local = jnp.concatenate(
        [
            grad_gain_one,
            grad_bias_one,
            grad_gain_two,
            grad_bias_two,
            projected_sums[0],
            projected_sums[2],
            jnp.sum(grad_branch.astype(jnp.float32), axis=0),
            jnp.sum(upstream, axis=0),
            jnp.sum(grad_expanded.astype(jnp.float32), axis=0),
        ]
    )
    shard_grads = (
        lax.psum_scatter(grad_input, ("batch", "head"), scatter_dimension=0, tiled=True),
        lax.psum_scatter(grad_output, ("batch", "head"), scatter_dimension=0, tiled=True),
        lax.psum_scatter(grad_expand, ("batch", "head"), scatter_dimension=0, tiled=True),
        lax.psum_scatter(grad_contract, ("batch", "head"), scatter_dimension=0, tiled=True),
    )
    vector_grads = lax.psum(vector_local, ("batch", "head"))
    masters = (input_weight, output_weight, expand_weight, contract_weight)
    firsts = (input_first, output_first, expand_first, contract_first)
    seconds = (input_second, output_second, expand_second, contract_second)
    local_grad_sq = jnp.sum(
        jnp.stack([jnp.sum(piece_grad * piece_grad) for piece_grad in shard_grads])
    )
    weight_sq = jnp.stack([jnp.sum(master * master) for master in masters])
    grad_total = lax.psum(local_grad_sq, ("batch", "head"))
    grad_norm = jnp.sqrt(grad_total + jnp.sum(vector_grads * vector_grads))
    clip_factor = jnp.minimum(1.0, 1.0 / grad_norm)
    updated = [
        adam_direction(piece_grad, first_old, second_old, master, clip_factor)
        for piece_grad, first_old, second_old, master in zip(shard_grads, firsts, seconds, masters)
    ]
    update_sq = jnp.stack([jnp.sum(entry[2] * entry[2]) for entry in updated])
    weight_total, update_total = lax.psum((weight_sq, update_sq), ("batch", "head"))
    weight_norms = jnp.sqrt(weight_total)
    update_norms = jnp.sqrt(update_total)
    matrix_norms = jnp.concatenate([weight_norms, update_norms])
    results = []
    for position in range(4):
        first_new, second_new, direction = updated[position]
        new_master = (
            masters[position]
            - MATRIX_RATE * (weight_norms[position] / update_norms[position]) * direction
        )
        results.append((first_new, second_new, new_master, new_master.astype(jnp.bfloat16)))
    vector_first_new, vector_second_new, vector_direction = adam_direction(
        vector_grads, vector_first, vector_second, vector_params, clip_factor
    )
    vector_new = vector_params - VECTOR_RATE * vector_direction
    return (
        block_out,
        input_grad,
        grad_norm,
        matrix_norms,
        results[0][0],
        results[0][1],
        results[0][2],
        results[0][3],
        results[1][0],
        results[1][1],
        results[1][2],
        results[1][3],
        results[2][0],
        results[2][1],
        results[2][2],
        results[2][3],
        results[3][0],
        results[3][1],
        results[3][2],
        results[3][3],
        vector_first_new,
        vector_second_new,
        vector_new,
    )


def solution(mesh):
    placed = (
        P(("batch", "head"), None),
        P(("batch", "head"), None),
        P("batch", None),
        P(("batch", "head"), None),
        P(("batch", "head"), None),
        P(("batch", "head"), None),
        P(("batch", "head"), None),
        P(),
        P(("batch", "head"), None),
        P(("batch", "head"), None),
        P(("batch", "head"), None),
        P(("batch", "head"), None),
        P(("batch", "head"), None),
        P(("batch", "head"), None),
        P(("batch", "head"), None),
        P(("batch", "head"), None),
        P(),
        P(),
    )
    return jax.shard_map(
        on_device,
        mesh=mesh,
        in_specs=placed,
        out_specs=(
            P(("batch", "head"), None),
            P(("batch", "head"), None),
            P(),
            P(),
            P(("batch", "head"), None),
            P(("batch", "head"), None),
            P(("batch", "head"), None),
            P(("batch", "head"), None),
            P(("batch", "head"), None),
            P(("batch", "head"), None),
            P(("batch", "head"), None),
            P(("batch", "head"), None),
            P(("batch", "head"), None),
            P(("batch", "head"), None),
            P(("batch", "head"), None),
            P(("batch", "head"), None),
            P(("batch", "head"), None),
            P(("batch", "head"), None),
            P(("batch", "head"), None),
            P(("batch", "head"), None),
            P(),
            P(),
            P(),
        ),
        check_vma=False,
    )
```

profile of v0, /device:TPU:0, one launch (start us, length us, event | category | flops | bytes accessed | tf_op | source)
XLA Modules:
  0.0 1045.3 jit_solution(83864289830116474)
XLA Ops:
  17.2 57.2 %all-gather.5.cloned.1.call-done = bf16[2304,768]{1,0:T(8,128)(2,1)} async-done(((bf16[72,768]{1,0:T(8,128)(2,1)}), bf16[2304,768]{1,0:T(8,128)(2,1)}) %all-gather.5.cloned.1.call-update) | async-done | bytes 3538960 | tf_op jit(solution)/shard_map/all_gather | solution.py:173
  91.0 35.5 %all-to-all-done = bf16[3,512,768]{1,0,2:T(4,128)(2,1)S(1)} async-done(((bf16[3,512,768]{1,0,2:T(4,128)(2,1)}), bf16[3,512,768]{1,0,2:T(4,128)(2,1)S(1)}, u32[]{:S(2)}, u32[]{:S(2)}) %all-to-all-start) | async-done | bytes 2359328 | tf_op jit(solution)/shard_map/all_to_all | solution.py:191
  130.9 90.2 %while.27 = (s32[]{:T(128)}, bf16[4,512,3,64]{1,3,2,0:T(8,128)(2,1)}, f32[4,3,512,1]{2,1,3,0:T(4,128)S(1)}, s32[4]{0:T(128)S(1)}, s32[2048]{0:T(1024)S(1)}, /*in...) while((s32[]{:T(128)}, ...), condition=%wide.region_8.9_spmd, body=%wide.region_5.8_spmd.sunk | while | flops 846298112 | bytes 43983052 | solution.py:62
  168.7 7.3 fusion.142
  191.2 7.3 fusion.142
  213.8 7.3 fusion.142
  226.2 12.5 %all-to-all-done.1 = bf16[4,512,192]{1,2,0:T(8,128)(2,1)} async-done(((bf16[4,512,192]{1,2,0:T(8,128)(2,1)}), bf16[4,512,192]{1,2,0:T(8,128)(2,1)}, u32[]{:S(2)}, u32[]{:S(2)}) %all-to-all-start.1) | async-done | bytes 786464 | tf_op jit(solution)/shard_map/all_to_all | solution.py:193
  242.7 8.6 fusion.72
  251.4 13.3 %all-gather.11.cloned.1.call-done = bf16[768,3072]{1,0:T(8,128)(2,1)} async-done(((bf16[24,3072]{1,0:T(8,128)(2,1)}), bf16[768,3072]{1,0:T(8,128)(2,1)}) %all-gather.11.cloned.1.call-update) | async-done | bytes 4718608 | tf_op jit(solution)/shard_map/all_gather | solution.py:176
  264.7 10.3 convert_reduce_fusion
  291.2 7.9 all-to-all-done.2
  303.4 140.5 %while.28 = (s32[]{:T(128)}, f32[2048,3,64]{0,2,1:T(8,128)}, f32[2048,3,64]{0,2,1:T(8,128)}, bf16[4,512,3,64]{1,3,2,0:T(8,128)(2,1)}, s32[4]{0:T(128)S(1)}, /*in...) while((s32[]{:T(128)}, f32[2048,3,64]{0,2,1:T(8,128)}, ...), condition=%wide.region_15.16_spmd.clone, body=%wide.region_13.15_spmd.clone.sunk | while | flops 2065660928 | bytes 219607728 | solution.py:109
  309.7 7.3 multiply_reduce_fusion.18
  455.0 53.8 %all_to_all.68 = bf16[3,2048,192]{2,0,1:T(4,128)(2,1)} all-to-all(bf16[3,2048,192]{2,0,1:T(4,128)(2,1)} %copy.155), channel_id=1, replica_groups=mesh['batch'=8,'head'=4] {'head'}, dimensions={1} | all-to-all | bytes 4718592 | tf_op jit(solution)/shard_map/all_to_all | solution.py:237
  520.8 10.0 convolution_bitcast_fusion
  530.9 9.9 copy.165
  542.3 8.5 fusion.71
  550.7 7.5 copy.163
  569.5 68.4 %reduce-scatter.7.cloned.1.call-done = f32[72,768]{1,0:T(8,128)} async-done(((f32[2304,768]{1,0:T(8,128)}), f32[72,768]{1,0:T(8,128)}) %reduce-scatter.7.cloned.1.call-update) | async-done | bytes 221200 | tf_op jit(solution)/shard_map/reduce_scatter | solution.py:264
  640.8 137.8 %reduce-scatter.13.cloned.1.call-done = f32[24,3072]{1,0:T(8,128)} async-done(((f32[768,3072]{1,0:T(8,128)}), f32[24,3072]{1,0:T(8,128)}) %reduce-scatter.13.cloned.1.call-update) | async-done | bytes 294928 | tf_op jit(solution)/shard_map/reduce_scatter | solution.py:267
  781.0 138.9 %reduce-scatter.11.cloned.1.call-done = f32[96,768]{1,0:T(8,128)} async-done(((f32[3072,768]{1,0:T(8,128)}), f32[96,768]{1,0:T(8,128)}) %reduce-scatter.11.cloned.1.call-update) | async-done | bytes 294928 | tf_op jit(solution)/shard_map/reduce_scatter | solution.py:266
  923.0 9.2 add_convert_fusion.2
  932.2 40.5 %all-reduce.1 = (f32[]{:T(128)}, f32[9216]{0:T(1024)S(1)}) all-reduce(f32[]{:T(128)S(6)} %reduce_sum.388, f32[9216]{0:T(1024)S(1)} %constant_dynamic-update-slice_fusion), channel_id=1, replica_groups=mesh['batch'=8,'head'=4] {'batch','head'}, use_global_device_ids=true, to_apply=%region_26.27 | all-reduce | flops 9217 | bytes 73736 | tf_op jit(solution)/shard_map/psum | solution.py:277
  986.5 39.3 %all-reduce = (f32[4]{0:T(128)S(1)}, f32[4]{0:T(128)S(1)}) all-reduce(f32[4]{0:T(128)S(1)} %get-tuple-element.418, f32[4]{0:T(128)S(1)} %get-tuple-element.417), channel_id=1, replica_groups=mesh['batch'=8,'head'=4] {'batch','head'}, use_global_device_ids=true, to_apply=%region_46.47 | all-reduce | flops 8 | bytes 64 | tf_op jit(solution)/shard_map/psum | solution.py:285
  (451 shorter events, 314.1 us)
Async XLA Ops:
  7.2 67.2 %all-gather.5.cloned.1.call-start = ((), (), s32[]{:S(2)}) async-start(), calls=%async_computation.8 | async-start | bytes 3649536 | tf_op jit(solution)/shard_map/all_gather | solution.py:173
  8.9 217.4 %all-gather.7.cloned.1.call-start = ((), (), s32[]{:S(2)}) async-start(), calls=%async_computation.9 | async-start | bytes 1216512 | tf_op jit(solution)/shard_map/all_gather | solution.py:174
  10.4 232.3 %all-gather.9.cloned.1.call-start = ((), (), s32[]{:S(2)}) async-start(), calls=%async_computation.10 | async-start | bytes 4866048 | tf_op jit(solution)/shard_map/all_gather | solution.py:175
  13.6 65.2 %copy-start.49 = (f32[768]{0:T(1024)}, f32[768]{0:T(1024)S(1)}, u32[]{:S(2)}) copy-start(f32[768]{0:T(1024)S(1)} %get-tuple-element.403) | copy-start | bytes 9220
  13.6 65.2 %copy-start.74 = (f32[768]{0:T(1024)}, f32[768]{0:T(1024)S(1)}, u32[]{:S(2)}) copy-start(f32[768]{0:T(1024)S(1)} %get-tuple-element.402) | copy-start | bytes 9220
  15.0 63.8 %copy-start.53 = (f32[512]{0:T(512)}, f32[512]{0:T(512)S(1)}, u32[]{:S(2)}) copy-start(f32[512]{0:T(512)S(1)} %broadcast_multiply_fusion.1) | copy-start | bytes 6148
  17.1 61.7 %copy-start.55 = (f32[512]{0:T(512)}, f32[512]{0:T(512)S(1)}, u32[]{:S(2)}) copy-start(f32[512]{0:T(512)S(1)} %fusion.65) | copy-start | bytes 6148
  83.2 43.4 %all-to-all-start = ((bf16[3,512,768]{1,0,2:T(4,128)(2,1)}), bf16[3,512,768]{1,0,2:T(4,128)(2,1)S(1)}, u32[]{:S(2)}, u32[]{:S(2)}) async-start(bf16[3,512,768]{1,0,2:T(4,128)(2,1)} %copy.147), calls=%async_computation | async-start | bytes 6291456 | tf_op jit(solution)/shard_map/all_to_all | solution.py:191
  87.0 177.7 %all-gather.11.cloned.1.call-start = ((), (), s32[]{:S(2)}) async-start(), calls=%async_computation.11 | async-start | bytes 4866048 | tf_op jit(solution)/shard_map/all_gather | solution.py:176
  130.9 107.8 %copy-start.9 = (bf16[512,768]{1,0:T(8,128)(2,1)S(1)}, bf16[512,768]{1,0:T(8,128)(2,1)}, u32[]{:S(2)}) copy-start(bf16[512,768]{1,0:T(8,128)(2,1)} %param.22) | copy-start | bytes 2359300
  130.9 107.8 %copy-start.76 = (f32[768]{0:T(1024)S(1)}, f32[768]{0:T(1024)}, u32[]{:S(2)}) copy-start(f32[768]{0:T(1024)} %get-tuple-element.399) | copy-start | bytes 9220
  221.1 17.6 %all-to-all-start.1 = ((bf16[4,512,192]{1,2,0:T(8,128)(2,1)}), bf16[4,512,192]{1,2,0:T(8,128)(2,1)}, u32[]{:S(2)}, u32[]{:S(2)}) async-start(bf16[4,512,192]{1,2,0:T(8,128)(2,1)} %bitcast.161), calls=%async_computation.1 | async-start | bytes 1572864 | tf_op jit(solution)/shard_map/all_to_all | solution.py:193
  284.0 15.1 %all-to-all-start.2 = ((bf16[512,4,192]{0,2,1:T(8,128)(2,1)}), bf16[512,4,192]{0,2,1:T(8,128)(2,1)S(1)}, u32[]{:S(2)}, u32[]{:S(2)}) async-start(bf16[512,4,192]{0,2,1:T(8,128)(2,1)} %bitcast.156), calls=%async_computation.2 | async-start | bytes 1572864 | tf_op jit(solution)/shard_map/all_to_all | solution.py:233
  287.5 280.4 %reduce-scatter.9.cloned.1.call-start = ((), (), s32[]{:S(2)}) async-start(), calls=%async_computation.13 | async-start | bytes 2433024 | tf_op jit(solution)/shard_map/reduce_scatter | solution.py:265
  291.1 346.7 %reduce-scatter.7.cloned.1.call-start = ((), (), s32[]{:S(2)}) async-start(), calls=%async_computation.12 | async-start | bytes 7299072 | tf_op jit(solution)/shard_map/reduce_scatter | solution.py:264
  519.7 258.9 %reduce-scatter.13.cloned.1.call-start = ((), (), s32[]{:S(2)}) async-start(), calls=%async_computation.15 | async-start | bytes 9732096 | tf_op jit(solution)/shard_map/reduce_scatter | solution.py:267
  540.8 379.1 %reduce-scatter.11.cloned.1.call-start = ((), (), s32[]{:S(2)}) async-start(), calls=%async_computation.14 | async-start | bytes 9732096 | tf_op jit(solution)/shard_map/reduce_scatter | solution.py:266
  567.8 355.1 %copy-start.16 = (f32[512,768]{1,0:T(8,128)S(1)}, f32[512,768]{1,0:T(8,128)}, u32[]{:S(2)}) copy-start(f32[512,768]{1,0:T(8,128)} %copy-done.13) | copy-start | bytes 4718596
  567.8 355.1 %copy-start.71 = (f32[768]{0:T(1024)S(1)}, f32[768]{0:T(1024)}, u32[]{:S(2)}) copy-start(f32[768]{0:T(1024)} %get-tuple-element.404) | copy-start | bytes 9220
  932.2 100.8 %copy-start.46 = (f32[9216]{0:T(1024)S(1)}, f32[9216]{0:T(1024)}, u32[]{:S(2)}) copy-start(f32[9216]{0:T(1024)} %param.29) | copy-start | bytes 110596
  932.2 100.8 %copy-start.51 = (f32[9216]{0:T(1024)S(1)}, f32[9216]{0:T(1024)}, u32[]{:S(2)}) copy-start(f32[9216]{0:T(1024)} %param.39) | copy-start | bytes 110596
  972.8 60.3 %copy-start.52 = (f32[9216]{0:T(1024)S(1)}, f32[9216]{0:T(1024)}, u32[]{:S(2)}) copy-start(f32[9216]{0:T(1024)} %param.38) | copy-start | bytes 110596
  976.6 59.6 %copy-start.30 = (f32[24,3072]{1,0:T(8,128)}, f32[24,3072]{1,0:T(8,128)S(1)}, u32[]{:S(2)}) copy-start(f32[24,3072]{1,0:T(8,128)S(1)} %get-tuple-element.378) | copy-start | bytes 884740
  976.6 59.6 %copy-start.31 = (f32[24,3072]{1,0:T(8,128)}, f32[24,3072]{1,0:T(8,128)S(1)}, u32[]{:S(2)}) copy-start(f32[24,3072]{1,0:T(8,128)S(1)} %get-tuple-element.379) | copy-start | bytes 884740
  (114 other events, 1502.3 us)
Sparse Core Ops, SparseCore 0:
  11.5 62.8 all-gather.4
  77.9 54.3 all-gather.6
  135.7 62.6 all-gather.8
  201.7 62.9 all-gather.10
  293.3 99.1 reduce-scatter.8
  519.9 117.9 reduce-scatter.6
  643.8 134.7 reduce-scatter.12
  785.5 134.4 reduce-scatter.10
where the time goes:
time: 1050 us
  waiting for transfers between devices  472 us (45%)
  matrix products  220 us (21%)
  blocking collectives  134 us (13%)
  other arithmetic  110 us (10%)
  local copies, waits for them, and re-layouts  64.5 us (6%)
  between operations  25.8 us (2%)
  starting transfers between devices  12.5 us (1%)
    reduce_scatter x1, waiting for transfers between devices, on_device(): lax.psum_scatter(grad_expand, ('batch', 'head'), scatter_dimension=0, til...  139 us
    reduce_scatter x1, waiting for transfers between devices, on_device(): lax.psum_scatter(grad_contract, ('batch', 'head'), scatter_dimension=0, t...  138 us
    reduce_scatter x1, waiting for transfers between devices, on_device(): lax.psum_scatter(grad_input, ('batch', 'head'), scatter_dimension=0, tile...  68.4 us
    all_gather x1, waiting for transfers between devices, on_device(): lax.all_gather(input_weight.astype(jnp.bfloat16), ('batch', 'head'), axis...  57.2 us
    all_to_all x1, blocking collectives, on_device(): lax.all_to_all(grad_projected_heads, 'head', split_axis=1, concat_axis=2,...  53.8 us
    psum x1, blocking collectives, on_device(): grad_total = lax.psum(local_grad_sq, ('batch', 'head'))  40.5 us
    psum x1, blocking collectives, on_device(): lax.psum((weight_sq, update_sq), ('batch', 'head'))  39.3 us
    all_to_all x1, waiting for transfers between devices, on_device(): lax.all_to_all(projected, 'head', split_axis=2, concat_axis=1, tiled=True)  35.5 us
  transfers between devices with their start and end apart: 11, of which 8 were waited for; matrix products, arithmetic and copies ran while one was open for 32% of the time, Pallas kernels for 0%

commit v1 on v0

--- a/solution.py
+++ b/solution.py
@@ -234,8 +234,14 @@
     grad_projected_heads = head_backward(
         head_inputs, grad_heads, log_totals, segment, block_count, block_rows, score_scale
     )
-    grad_projected = lax.all_to_all(
-        grad_projected_heads, "head", split_axis=1, concat_axis=2, tiled=True
+    grad_projected = jnp.concatenate(
+        lax.all_to_all(
+            jnp.stack(jnp.split(grad_projected_heads, lax.axis_size("head"), 1), axis=0),
+            "head",
+            0,
+            0,
+        ),
+        2,
     )
     grad_input = jnp.einsum(
         "cto,td->cod", grad_projected, normed_one, preferred_element_type=jnp.float32

time: 1050 us -> 1020 us (0.971)
  blocking collectives: 134 us -> 111 us
  local copies, waits for them, and re-layouts: 64.5 us -> 47.3 us
    all_to_all x1, blocking collectives: 53.8 us -> 31 us  [on_device(): lax.all_to_all(jnp.stack(jnp.split(grad_projected_heads, lax.axis_size('h...]
    all_to_all x2 -> x0, local copies, waits for them, and re-layouts: 13.1 us -> none  [on_device(): lax.all_to_all(grad_projected_heads, 'head', split_axis=1, concat_axis=2,...]
  transfers between devices with their start and end apart: 11 -> 11, of which waited for: 8 -> 8; matrix products, arithmetic and copies ran while one was open for 32% -> 31% of each run, Pallas kernels for 0% -> 0%
where the time goes in v1:
time: 1020 us; the launch traced here: 1010 us
  waiting for transfers between devices  480 us (47%)
  matrix products  221 us (22%)
  blocking collectives  111 us (11%)
  other arithmetic  107 us (10%)
  local copies, waits for them, and re-layouts  47.3 us (5%)
  between operations  25.7 us (3%)
  starting transfers between devices  12.8 us (1%)
    reduce_scatter x1, waiting for transfers between devices, on_device(): lax.psum_scatter(grad_expand, ('batch', 'head'), scatter_dimension=0, til...  139 us
    reduce_scatter x1, waiting for transfers between devices, on_device(): lax.psum_scatter(grad_contract, ('batch', 'head'), scatter_dimension=0, t...  138 us
    reduce_scatter x1, waiting for transfers between devices, on_device(): lax.psum_scatter(grad_input, ('batch', 'head'), scatter_dimension=0, tile...  76.6 us
    all_gather x1, waiting for transfers between devices, on_device(): lax.all_gather(input_weight.astype(jnp.bfloat16), ('batch', 'head'), axis...  57.2 us
    psum x1, blocking collectives, on_device(): grad_total = lax.psum(local_grad_sq, ('batch', 'head'))  40.9 us
    psum x1, blocking collectives, on_device(): lax.psum((weight_sq, update_sq), ('batch', 'head'))  39.3 us
    all_to_all x1, waiting for transfers between devices, on_device(): lax.all_to_all(projected, 'head', split_axis=2, concat_axis=1, tiled=True)  35.8 us
    dot_general x8, matrix products, masked_scores(): jnp.einsum('qhd,khd->hqk', query_block, key_rows, preferred_element_type=...  31.5 us
  transfers between devices with their start and end apart: 11, of which 8 were waited for; matrix products, arithmetic and copies ran while one was open for 31% of the time, Pallas kernels for 0%

profile of v1, /device:TPU:0, one launch (start us, length us, event | category | flops | bytes accessed | tf_op | source)
XLA Modules:
  0.0 1012.2 jit_solution(7820720820823793373)
XLA Ops:
  17.2 57.2 %all-gather.5.cloned.1.call-done = bf16[2304,768]{1,0:T(8,128)(2,1)} async-done(((bf16[72,768]{1,0:T(8,128)(2,1)}), bf16[2304,768]{1,0:T(8,128)(2,1)}) %all-gather.5.cloned.1.call-update) | async-done | bytes 3538960 | tf_op jit(solution)/shard_map/all_gather | solution.py:173
  90.8 35.8 %all-to-all-done = bf16[3,512,768]{1,0,2:T(4,128)(2,1)S(1)} async-done(((bf16[3,512,768]{1,0,2:T(4,128)(2,1)}), bf16[3,512,768]{1,0,2:T(4,128)(2,1)S(1)}, u32[]{:S(2)}, u32[]{:S(2)}) %all-to-all-start) | async-done | bytes 2359328 | tf_op jit(solution)/shard_map/all_to_all | solution.py:191
  130.9 90.3 %while.27 = (s32[]{:T(128)}, bf16[4,512,3,64]{1,3,2,0:T(8,128)(2,1)}, f32[4,3,512,1]{2,1,3,0:T(4,128)S(1)}, s32[4]{0:T(128)S(1)}, s32[2048]{0:T(1024)S(1)}, /*in...) while((s32[]{:T(128)}, ...), condition=%wide.region_8.9_spmd, body=%wide.region_5.8_spmd.sunk | while | flops 846298112 | bytes 43983052 | solution.py:62
  146.1 7.3 fusion.141
  168.7 7.3 fusion.141
  191.2 7.4 fusion.141
  213.8 7.3 fusion.141
  226.6 12.2 %all-to-all-done.1 = bf16[4,512,192]{1,2,0:T(8,128)(2,1)} async-done(((bf16[4,512,192]{1,2,0:T(8,128)(2,1)}), bf16[4,512,192]{1,2,0:T(8,128)(2,1)}, u32[]{:S(2)}, u32[]{:S(2)}) %all-to-all-start.1) | async-done | bytes 786464 | tf_op jit(solution)/shard_map/all_to_all | solution.py:193
  242.8 8.6 fusion.72
  251.4 13.3 %all-gather.11.cloned.1.call-done = bf16[768,3072]{1,0:T(8,128)(2,1)} async-done(((bf16[24,3072]{1,0:T(8,128)(2,1)}), bf16[768,3072]{1,0:T(8,128)(2,1)}) %all-gather.11.cloned.1.call-update) | async-done | bytes 4718608 | tf_op jit(solution)/shard_map/all_gather | solution.py:176
  264.7 10.3 %convert_reduce_fusion = (f32[3072]{0:T(1024)}, bf16[512,3072]{1,0:T(8,128)(2,1)S(1)}) fusion(f32[512,3072]{1,0:T(8,128)} %fusion.72, f32[3072]{0:T(1024)S(1)} %slice.92, bf16[512,768]{1,0:T(8,128)(2,1)S(1)} %copy-done.16, bf16[768,3072]{1,0:T(8,128)(2,1)} %all-gather.11.cloned.1.call-done), kind=kOutput, calls=%fused_computation.57 | convolution fusion | flops 2452091904 | bytes 14966784 | tf_op jit(solution)/shard_map/to,of->tf/dot_general | solution.py:214
  291.2 7.9 all-to-all-done.2
  303.4 140.8 %while.28 = (s32[]{:T(128)}, f32[2048,3,64]{0,2,1:T(8,128)}, f32[2048,3,64]{0,2,1:T(8,128)}, bf16[4,512,3,64]{1,3,2,0:T(8,128)(2,1)}, s32[4]{0:T(128)S(1)}, /*in...) while((s32[]{:T(128)}, f32[2048,3,64]{0,2,1:T(8,128)}, ...), condition=%wide.region_15.16_spmd.clone, body=%wide.region_13.15_spmd.clone.sunk | while | flops 2065660928 | bytes 219607728 | solution.py:109
  309.5 7.4 multiply_reduce_fusion.18
  448.3 31.0 %all_to_all.55 = bf16[4,3,512,192]{2,3,1,0:T(8,128)(2,1)S(1)} all-to-all(bf16[4,3,512,192]{2,3,1,0:T(8,128)(2,1)S(1)} %pad_maximum_fusion.1), channel_id=1, replica_groups=mesh['batch'=8,'head'=4] {'head'}, dimensions={0} | all-to-all | bytes 4718592 | tf_op jit(solution)/shard_map/all_to_all | solution.py:238
  486.9 10.3 %convolution_bitcast_fusion = f32[768,3072]{0,1:T(8,128)} fusion(bf16[512,768]{1,0:T(8,128)(2,1)} %param.23, f32[512,3072]{1,0:T(8,128)} %fusion.72, f32[3072]{0:T(1024)S(1)} %copy-done.65), kind=kOutput, calls=%fused_computation.59 | convolution fusion | flops 2431647744 | bytes 16527360 | tf_op jit(solution)/shard_map/to,tf->of/dot_general | solution.py:211
  497.2 9.9 copy.136
  507.9 9.0 fusion.71
  527.7 76.6 %reduce-scatter.7.cloned.1.call-done = f32[72,768]{1,0:T(8,128)} async-done(((f32[2304,768]{1,0:T(8,128)}), f32[72,768]{1,0:T(8,128)}) %reduce-scatter.7.cloned.1.call-update) | async-done | bytes 221200 | tf_op jit(solution)/shard_map/reduce_scatter | solution.py:270
  607.2 137.9 %reduce-scatter.13.cloned.1.call-done = f32[24,3072]{1,0:T(8,128)} async-done(((f32[768,3072]{1,0:T(8,128)}), f32[24,3072]{1,0:T(8,128)}) %reduce-scatter.13.cloned.1.call-update) | async-done | bytes 294928 | tf_op jit(solution)/shard_map/reduce_scatter | solution.py:273
  747.5 138.9 %reduce-scatter.11.cloned.1.call-done = f32[96,768]{1,0:T(8,128)} async-done(((f32[3072,768]{1,0:T(8,128)}), f32[96,768]{1,0:T(8,128)}) %reduce-scatter.11.cloned.1.call-update) | async-done | bytes 294928 | tf_op jit(solution)/shard_map/reduce_scatter | solution.py:272
  889.5 9.2 add_convert_fusion.2
  898.7 40.9 %all-reduce.1 = (f32[]{:T(128)}, f32[9216]{0:T(1024)S(1)}) all-reduce(f32[]{:T(128)S(6)} %reduce_sum.388, f32[9216]{0:T(1024)S(1)} %constant_dynamic-update-slice_fusion), channel_id=1, replica_groups=mesh['batch'=8,'head'=4] {'batch','head'}, use_global_device_ids=true, to_apply=%region_26.27 | all-reduce | flops 9217 | bytes 73736 | tf_op jit(solution)/shard_map/psum | solution.py:283
  953.5 39.3 %all-reduce = (f32[4]{0:T(128)S(1)}, f32[4]{0:T(128)S(1)}) all-reduce(f32[4]{0:T(128)S(1)} %get-tuple-element.399, f32[4]{0:T(128)S(1)} %get-tuple-element.398), channel_id=1, replica_groups=mesh['batch'=8,'head'=4] {'batch','head'}, use_global_device_ids=true, to_apply=%region_46.47 | all-reduce | flops 8 | bytes 64 | tf_op jit(solution)/shard_map/psum | solution.py:291
  (445 shorter events, 294.8 us)
Async XLA Ops:
  7.2 67.2 %all-gather.5.cloned.1.call-start = ((), (), s32[]{:S(2)}) async-start(), calls=%async_computation.8 | async-start | bytes 3649536 | tf_op jit(solution)/shard_map/all_gather | solution.py:173
  8.9 217.7 %all-gather.7.cloned.1.call-start = ((), (), s32[]{:S(2)}) async-start(), calls=%async_computation.9 | async-start | bytes 1216512 | tf_op jit(solution)/shard_map/all_gather | solution.py:174
  10.4 232.3 %all-gather.9.cloned.1.call-start = ((), (), s32[]{:S(2)}) async-start(), calls=%async_computation.10 | async-start | bytes 4866048 | tf_op jit(solution)/shard_map/all_gather | solution.py:175
  13.6 65.2 %copy-start.47 = (f32[768]{0:T(1024)}, f32[768]{0:T(1024)S(1)}, u32[]{:S(2)}) copy-start(f32[768]{0:T(1024)S(1)} %get-tuple-element.384) | copy-start | bytes 9220
  13.6 65.2 %copy-start.72 = (f32[768]{0:T(1024)}, f32[768]{0:T(1024)S(1)}, u32[]{:S(2)}) copy-start(f32[768]{0:T(1024)S(1)} %get-tuple-element.383) | copy-start | bytes 9220
  15.0 63.8 %copy-start.51 = (f32[512]{0:T(512)}, f32[512]{0:T(512)S(1)}, u32[]{:S(2)}) copy-start(f32[512]{0:T(512)S(1)} %broadcast_multiply_fusion.1) | copy-start | bytes 6148
  17.1 61.7 %copy-start.53 = (f32[512]{0:T(512)}, f32[512]{0:T(512)S(1)}, u32[]{:S(2)}) copy-start(f32[512]{0:T(512)S(1)} %fusion.65) | copy-start | bytes 6148
  83.1 43.4 %all-to-all-start = ((bf16[3,512,768]{1,0,2:T(4,128)(2,1)}), bf16[3,512,768]{1,0,2:T(4,128)(2,1)S(1)}, u32[]{:S(2)}, u32[]{:S(2)}) async-start(bf16[3,512,768]{1,0,2:T(4,128)(2,1)} %copy.124), calls=%async_computation | async-start | bytes 6291456 | tf_op jit(solution)/shard_map/all_to_all | solution.py:191
  87.0 177.7 %all-gather.11.cloned.1.call-start = ((), (), s32[]{:S(2)}) async-start(), calls=%async_computation.11 | async-start | bytes 4866048 | tf_op jit(solution)/shard_map/all_gather | solution.py:176
  130.9 107.9 %copy-start.9 = (bf16[512,768]{1,0:T(8,128)(2,1)S(1)}, bf16[512,768]{1,0:T(8,128)(2,1)}, u32[]{:S(2)}) copy-start(bf16[512,768]{1,0:T(8,128)(2,1)} %param.22) | copy-start | bytes 2359300
  130.9 107.9 %copy-start.74 = (f32[768]{0:T(1024)S(1)}, f32[768]{0:T(1024)}, u32[]{:S(2)}) copy-start(f32[768]{0:T(1024)} %get-tuple-element.380) | copy-start | bytes 9220
  221.2 17.6 %all-to-all-start.1 = ((bf16[4,512,192]{1,2,0:T(8,128)(2,1)}), bf16[4,512,192]{1,2,0:T(8,128)(2,1)}, u32[]{:S(2)}, u32[]{:S(2)}) async-start(bf16[4,512,192]{1,2,0:T(8,128)(2,1)} %bitcast.165), calls=%async_computation.1 | async-start | bytes 1572864 | tf_op jit(solution)/shard_map/all_to_all | solution.py:193
  284.0 15.1 %all-to-all-start.2 = ((bf16[512,4,192]{0,2,1:T(8,128)(2,1)}), bf16[512,4,192]{0,2,1:T(8,128)(2,1)S(1)}, u32[]{:S(2)}, u32[]{:S(2)}) async-start(bf16[512,4,192]{0,2,1:T(8,128)(2,1)} %bitcast.160), calls=%async_computation.2 | async-start | bytes 1572864 | tf_op jit(solution)/shard_map/all_to_all | solution.py:233
  287.5 238.6 %reduce-scatter.9.cloned.1.call-start = ((), (), s32[]{:S(2)}) async-start(), calls=%async_computation.13 | async-start | bytes 2433024 | tf_op jit(solution)/shard_map/reduce_scatter | solution.py:271
  291.2 313.1 %reduce-scatter.7.cloned.1.call-start = ((), (), s32[]{:S(2)}) async-start(), calls=%async_computation.12 | async-start | bytes 7299072 | tf_op jit(solution)/shard_map/reduce_scatter | solution.py:270
  486.2 258.9 %reduce-scatter.13.cloned.1.call-start = ((), (), s32[]{:S(2)}) async-start(), calls=%async_computation.15 | async-start | bytes 9732096 | tf_op jit(solution)/shard_map/reduce_scatter | solution.py:273
  507.2 379.3 %reduce-scatter.11.cloned.1.call-start = ((), (), s32[]{:S(2)}) async-start(), calls=%async_computation.14 | async-start | bytes 9732096 | tf_op jit(solution)/shard_map/reduce_scatter | solution.py:272
  526.0 363.4 %copy-start.15 = (f32[512,768]{1,0:T(8,128)S(1)}, f32[512,768]{1,0:T(8,128)}, u32[]{:S(2)}) copy-start(f32[512,768]{1,0:T(8,128)} %copy-done.13) | copy-start | bytes 4718596
  526.0 363.4 %copy-start.69 = (f32[768]{0:T(1024)S(1)}, f32[768]{0:T(1024)}, u32[]{:S(2)}) copy-start(f32[768]{0:T(1024)} %get-tuple-element.385) | copy-start | bytes 9220
  898.7 101.2 %copy-start.44 = (f32[9216]{0:T(1024)S(1)}, f32[9216]{0:T(1024)}, u32[]{:S(2)}) copy-start(f32[9216]{0:T(1024)} %param.29) | copy-start | bytes 110596
  898.7 101.2 %copy-start.49 = (f32[9216]{0:T(1024)S(1)}, f32[9216]{0:T(1024)}, u32[]{:S(2)}) copy-start(f32[9216]{0:T(1024)} %param.39) | copy-start | bytes 110596
  939.7 60.3 %copy-start.50 = (f32[9216]{0:T(1024)S(1)}, f32[9216]{0:T(1024)}, u32[]{:S(2)}) copy-start(f32[9216]{0:T(1024)} %param.38) | copy-start | bytes 110596
  943.5 59.6 %copy-start.28 = (f32[24,3072]{1,0:T(8,128)}, f32[24,3072]{1,0:T(8,128)S(1)}, u32[]{:S(2)}) copy-start(f32[24,3072]{1,0:T(8,128)S(1)} %get-tuple-element.357) | copy-start | bytes 884740
  943.5 59.6 %copy-start.29 = (f32[24,3072]{1,0:T(8,128)}, f32[24,3072]{1,0:T(8,128)S(1)}, u32[]{:S(2)}) copy-start(f32[24,3072]{1,0:T(8,128)S(1)} %get-tuple-element.358) | copy-start | bytes 884740
  (112 other events, 1476.2 us)
Sparse Core Ops, SparseCore 0:
  11.5 62.8 all-gather.4
  77.9 54.3 all-gather.6
  135.7 62.6 all-gather.8
  201.7 62.9 all-gather.10
  293.3 99.1 reduce-scatter.8
  486.3 117.9 reduce-scatter.6
  610.2 134.8 reduce-scatter.12
  752.0 134.4 reduce-scatter.10
